TPU v7x, 32 devices: a whole 2x2x4 slice. The times are simulated.
32 devices in a mesh: lon: 4 (over x, core), frame: 8 (over z, y).
Axes of the slice: x: 2, y: 2, z: 4, core: 2. Of those that a mesh axis runs over, the one named last changes fastest.
Arguments:
- layer_input: bfloat16 [8, 16, 512, 128], P('frame', None, 'lon'), may hold values from -6 to 6
- hidden_saved: bfloat16 [8, 16, 512, 128], P('frame', None, 'lon'), as said below
- conv_weight: bfloat16 [3, 3, 128, 128], replicated, may hold values from -0.1875 to 0.1875
- queries: bfloat16 [2048, 128], P('lon'), may hold values from -6 to 6
- corr_cotangent: bfloat16 [8, 49, 2048], P('frame', None, 'lon'), may hold values from -0.59765625 to 0.59765625
- window_rows: int32 [8, 2048], P('frame', 'lon'), may hold values from 0 to 9
- window_cols: int32 [8, 2048], P('frame', 'lon'), may hold values from -3 to 124
- owner_strip: int32 [8, 2048, 1], P('frame', 'lon'), may hold values from 0 to 3; in each aligned block of 512 rows (0 to 511, 512 to 1023, ..., all dimensions but the last counted through in order) at most 128 rows name the same one
Outputs:
- query_grad: float32 [2048, 128], P(('lon', 'frame'))
- first_weight_grad: float32 [3, 3, 128, 128], replicated
- second_weight_grad: float32 [3, 3, 128, 128], replicated
Inputs may be any that keep to these rules, and one draw needn't show every extreme that they name: `hidden_saved`: rectifier outputs: zero or positive, a third or more of them exactly zero. `owner_strip`: in each frame, at most 128 of the 512 tracks homed on one strip name the same owning strip.
All inputs are finite; a program needn't handle non-finite values.
Results may differ from a plain program's by a relative error of at most 0.0045.
Values may be sent and summed in bfloat16 or wider, within the bound.
A program may use at most 64 MiB of HBM per device.

v0:
```python
import math
import jax
import jax.numpy as jnp
from jax import lax
from jax.sharding import PartitionSpec as P

WIN = 7


def padded_2(value, sides, width):
    for axis, dim in sides:
        peers, length = (lax.axis_size(axis), value.shape[dim])
        up = [(i, (i + 1) % peers) for i in range(peers)]
        down = [(j, i) for i, j in up]
        last = lax.slice_in_dim(value, length - width, length, axis=dim)
        first = lax.slice_in_dim(value, 0, width, axis=dim)
        before = lax.ppermute(last, axis, up)
        after = lax.ppermute(first, axis, down)
        value = jnp.concatenate([before, value, after], axis=dim)
    return value


def from_behind(value, axis, steps):
    count = lax.axis_size(axis)
    pairs = [(source, (source + steps) % count) for source in range(count)]
    return lax.ppermute(value, axis, pairs)


def pad_rows(field):
    return jnp.pad(field, ((1, 1), (0, 0), (0, 0)))


def conv_cells(padded, weight, out_cols):
    row_count = padded.shape[0] - 2
    result = jnp.zeros((row_count, out_cols, weight.shape[3]), jnp.float32)
    for row_tap in range(3):
        for col_tap in range(3):
            window = padded[row_tap : row_tap + row_count, col_tap : col_tap + out_cols]
            result = result + jnp.einsum(
                "rci,io->rco", window, weight[row_tap, col_tap], preferred_element_type=jnp.float32
            )
    return result


def conv_back(padded, weight, out_cols):
    row_count = padded.shape[0] - 2
    result = jnp.zeros((row_count, out_cols, weight.shape[2]), jnp.float32)
    for row_tap in range(3):
        for col_tap in range(3):
            window = padded[
                2 - row_tap : 2 - row_tap + row_count, 2 - col_tap : 2 - col_tap + out_cols
            ]
            result = result + jnp.einsum(
                "rco,io->rci", window, weight[row_tap, col_tap], preferred_element_type=jnp.float32
            )
    return result


def weight_terms(padded, grad):
    row_count, col_count, out_channels = grad.shape
    flat_grad = grad.reshape(row_count * col_count, out_channels)
    tap_terms = []
    for row_tap in range(3):
        for col_tap in range(3):
            window = padded[row_tap : row_tap + row_count, col_tap : col_tap + col_count].reshape(
                row_count * col_count, padded.shape[2]
            )
            tap_terms.append(
                lax.dot_general(
                    window, flat_grad, (((0,), (0,)), ((), ())), preferred_element_type=jnp.float32
                )
            )
    return jnp.stack(tap_terms).reshape(3, 3, padded.shape[2], out_channels)


def per_device(
    layer_input,
    hidden_saved,
    conv_weight,
    queries,
    corr_cotangent,
    window_rows,
    window_cols,
    owner_strip,
):
    strip_count = lax.axis_size("lon")
    input_local = layer_input[0]
    hidden_local = hidden_saved[0]
    row_count, col_count, channels = hidden_local.shape
    track_count = queries.shape[0]
    capacity = track_count // 4
    slot_count = strip_count * capacity
    wide_cols = col_count + 6
    taps_total = WIN * WIN
    reach = 4
    stacked = jnp.stack([input_local, hidden_local])
    edged = padded_2(stacked, (("lon", 2),), reach)
    input_edged = pad_rows(edged[0, :, reach - 1 : reach + col_count + 1])
    hidden_edged = pad_rows(edged[1, :, reach - 1 : reach + col_count + 1])
    feature_wide = conv_cells(pad_rows(edged[1]), conv_weight, wide_cols).astype(jnp.bfloat16)
    owners = owner_strip[0, :, 0]
    strip_ids = jnp.arange(strip_count, dtype=jnp.int32)
    marks = (owners[:, None] == strip_ids[None, :]).astype(jnp.int32)
    before = jnp.cumsum(marks, axis=0) - marks
    position = jnp.sum(before * marks, axis=1)
    slot_index = owners * capacity + position
    cot_rows = jnp.pad(corr_cotangent[0].T, ((0, 0), (0, 128 - taps_total)))
    meta_home = jnp.stack([window_rows[0], window_cols[0] + 3], axis=1)
    payload = jnp.concatenate([queries, cot_rows], axis=1)
    send_payload = (
        jnp.zeros((slot_count, payload.shape[1]), jnp.bfloat16).at[slot_index].set(payload)
    )
    send_meta = jnp.zeros((slot_count, meta_home.shape[1]), jnp.int32).at[slot_index].set(meta_home)
    got_payload, got_meta = (
        lax.all_to_all(send_payload, "lon", split_axis=0, concat_axis=0, tiled=True),
        lax.all_to_all(send_meta, "lon", split_axis=0, concat_axis=0, tiled=True),
    )
    query_slots = got_payload[:, :channels]
    cot_slots = got_payload[:, channels : channels + taps_total]
    block_rows = math.gcd(slot_count, 512)
    block_count = slot_count // block_rows
    feature_flat = feature_wide.reshape(row_count * wide_cols, channels)
    offsets = jnp.arange(WIN, dtype=jnp.int32)
    row_ids = jnp.arange(row_count, dtype=jnp.int32)
    col_ids = jnp.arange(wide_cols, dtype=jnp.int32)

    def block_step(grad_acc, block_items):
        cot_block, meta_block, query_block = block_items
        cot_square = cot_block.reshape(block_rows, WIN, WIN)
        row_hot = (
            meta_block[:, 0][:, None, None] + offsets[None, :, None] == row_ids[None, None, :]
        ).astype(jnp.bfloat16)
        col_hot = (
            meta_block[:, 1][:, None, None] + offsets[None, :, None] == col_ids[None, None, :]
        ).astype(jnp.bfloat16)
        placed_cols = jnp.einsum(
            "tij,tjh->tih", cot_square, col_hot, preferred_element_type=jnp.float32
        ).astype(jnp.bfloat16)
        spread = jnp.einsum(
            "tir,tih->trh", row_hot, placed_cols, preferred_element_type=jnp.float32
        ).astype(jnp.bfloat16)
        spread = spread.reshape(block_rows, row_count * wide_cols)
        block_grads = jnp.dot(spread, feature_flat, preferred_element_type=jnp.float32)
        grad_acc = grad_acc + lax.dot_general(
            spread, query_block, (((0,), (0,)), ((), ())), preferred_element_type=jnp.float32
        )
        return (grad_acc, block_grads)

    block_items = (
        cot_slots.reshape(block_count, block_rows, taps_total),
        got_meta.reshape(block_count, block_rows, got_meta.shape[1]),
        query_slots.reshape(block_count, block_rows, channels),
    )
    grad_flat, query_blocks = lax.scan(
        block_step, jnp.zeros((row_count * wide_cols, channels), jnp.float32), block_items
    )
    slot_grads = query_blocks.reshape(slot_count, channels)
    returned = lax.all_to_all(slot_grads, "lon", split_axis=0, concat_axis=0, tiled=True)
    home_grads = returned[slot_index]
    query_grad = lax.psum_scatter(home_grads, "frame", scatter_dimension=0, tiled=True)
    grad_wide = grad_flat.reshape(row_count, wide_cols, channels)
    from_prior = from_behind(grad_wide[:, col_count + 3 :], "lon", 1)
    from_next = from_behind(grad_wide[:, :3], "lon", -1)
    own_grad = grad_wide[:, 3 : col_count + 3]
    own_grad = own_grad.at[:, :3].add(from_prior)
    own_grad = own_grad.at[:, col_count - 3 :].add(from_next)
    grad_edged = padded_2(own_grad.astype(jnp.bfloat16), (("lon", 1),), 1)
    feature_grad = grad_edged[:, 1 : col_count + 1]
    hidden_grad = conv_back(pad_rows(grad_edged), conv_weight, col_count)
    pre_grad = jnp.where(hidden_local > 0, hidden_grad, jnp.zeros_like(hidden_grad)).astype(
        jnp.bfloat16
    )
    second_term = weight_terms(hidden_edged, feature_grad)
    first_term = weight_terms(input_edged, pre_grad)
    first_sum, second_sum = lax.psum((first_term, second_term), ("lon", "frame"))
    norm_factor = 1.0 / math.sqrt(row_count * col_count * strip_count * lax.axis_size("frame"))
    return (query_grad, first_sum * norm_factor, second_sum * norm_factor)


def solution(mesh):
    placed = (
        P("frame", None, "lon", None),
        P("frame", None, "lon", None),
        P(),
        P("lon", None),
        P("frame", None, "lon"),
        P("frame", "lon"),
        P("frame", "lon"),
        P("frame", "lon", None),
    )
    return jax.shard_map(
        per_device,
        mesh=mesh,
        in_specs=placed,
        out_specs=(P(("lon", "frame"), None), P(), P()),
        check_vma=False,
    )
```

profile of v0, /device:TPU:0, one launch (start us, length us, event | category | flops | bytes accessed | tf_op | source)
XLA Modules:
  0.0 221.2 jit_solution(16327299058159711779)
XLA Ops:
  8.0 0.8 fusion.142
  8.8 1.2 reduce-window.6
  10.5 0.7 fusion.141
  11.2 0.7 compare_select_fusion
  11.9 0.7 add_bitcast_fusion.1
  12.6 0.7 pad_add_fusion
  13.4 1.8 scatter_custom_fusion
  15.2 0.7 copy.76
  15.9 4.2 %all-to-all-start = ((s32[4,128,2]{1,2,0:T(2,128)}), s32[4,128,2]{1,2,0:T(2,128)S(1)}, u32[]{:S(2)}, u32[]{:S(2)}) async-start(s32[4,128,2]{1,2,0:T(2,128)} %copy.76), calls=%async_computation | async-start | bytes 8192 | tf_op jit(solution)/shard_map/all_to_all | solution.py:116
  20.3 1.8 collective-permute-start.1
  22.4 3.0 %scatter_custom_fusion.1 = bf16[512,256]{1,0:T(8,128)(2,1)} fusion(s32[512]{0:T(512)S(1)} %bitcast.248, bf16[512,256]{1,0:T(8,128)(2,1)S(1)} %copy.78, bf16[]{:T(256)} %constant.86.clone.1), kind=kCustom, calls=%fused_computation.147 | custom fusion | bytes 262146 | tf_op jit(solution)/shard_map/scatter | solution.py:111
  25.4 3.4 %all-to-all-start.1 = ((bf16[4,128,256]{2,1,0:T(8,128)(2,1)}), bf16[4,128,256]{2,1,0:T(8,128)(2,1)S(1)}, u32[]{:S(2)}, u32[]{:S(2)}) async-start(bf16[4,128,256]{2,1,0:T(8,128)(2,1)} %bitcast.13), calls=%async_computation.1 | async-start | bytes 524288 | tf_op jit(solution)/shard_map/all_to_all | solution.py:115
  29.3 0.5 pad_maximum_fusion
  29.9 0.9 copy-done.3
  30.8 0.4 fusion.44
  31.2 0.4 convolution_add_fusion.7
  31.6 0.4 convolution_add_fusion.6
  32.1 0.4 convolution_add_fusion.5
  32.5 0.4 convolution_add_fusion.4
  32.9 0.4 convolution_add_fusion.3
  33.4 0.4 convolution_add_fusion.2
  33.8 0.4 convolution_add_fusion.1
  34.2 1.3 fusion.9
  35.5 0.6 reshape.292
  36.1 5.9 %fusion.1 = bf16[512,16,134]{2,1,0:T(8,128)(2,1)} fusion(bf16[512,7,7]{2,1,0:T(8,128)(2,1)S(1)} %reshape.292, s32[512,7]{1,0:T(8,128)S(1)} %get-tuple-element.69, s32[512,7]{1,0:T(8,128)S(1)} %get-tuple-element.70), kind=kOutput, calls=%fused_computation.5 | convolution fusion | flops 23109632 | bytes 2274304 | tf_op jit(solution)/shard_map/while/body/eval_jaxpr/tir,tih->trh/dot_general | solution.py:139
  42.0 7.9 %copy.81 = bf16[512,16,134]{0,1,2:T(8,128)(2,1)} copy(bf16[512,16,134]{2,1,0:T(8,128)(2,1)} %fusion.1) | data formatting | bytes 4390912 | tf_op jit(solution)/shard_map/while/body/eval_jaxpr/tir,tih->trh/dot_general | solution.py:139
  49.9 2.8 %copy.83 = bf16[512,16,134]{0,2,1:T(8,128)(2,1)S(1)} copy(bf16[512,16,134]{0,1,2:T(8,128)(2,1)} %copy.81) | data formatting | bytes 4390912 | tf_op jit(solution)/shard_map/while/body/eval_jaxpr/convert_element_type | solution.py:141
  52.7 2.1 reshape.236
  54.9 2.6 %dot_general.141 = bf16[16,134,512]{2,1,0:T(8,128)(2,1)S(1)} reshape(bf16[2144,512]{1,0:T(8,128)(2,1)} %bitcast.235) | data formatting | bytes 4390912 | tf_op jit(solution)/shard_map/while/body/eval_jaxpr/dot_general | solution.py:144
  57.5 1.6 fusion.97
  59.2 0.5 collective-permute-start.2
  59.7 0.3 slice_bitcast_fusion
  60.2 1.3 collective-permute-start.3
  61.5 1.1 collective-permute-done.2
  63.7 1.8 collective-permute-start.5
  65.5 0.4 collective-permute-start.4
  65.9 0.3 fusion.20
  66.3 0.3 fusion.19
  66.6 0.3 fusion.18
  66.9 0.3 fusion.17
  67.3 0.4 fusion.16
  67.7 0.3 fusion.15
  68.0 0.3 fusion.14
  68.4 0.3 fusion.13
  68.7 0.3 fusion.12
  71.1 0.4 fusion.8
  71.8 0.7 copy-done.2
  73.2 0.3 fusion.28
  73.6 0.3 fusion.27
  73.9 0.3 fusion.26
  74.3 0.3 fusion.25
  74.6 0.3 fusion.24
  74.9 0.3 fusion.23
  75.3 0.3 fusion.22
  75.7 0.3 fusion.21
  76.0 0.8 copy-done.7
  76.8 0.6 copy-done
  77.5 2.5 %fusion.46 = f32[512,128,1]{1,0,2:T(8,128)} fusion(bf16[512,16,134]{0,1,2:T(8,128)(2,1)S(1)} %copy-done, bf16[16,134,128]{2,1,0:T(8,128)(2,1)} %fusion.9), kind=kOutput, calls=%fused_computation.87 | convolution fusion | flops 281018368 | bytes 3006464 | tf_op jit(solution)/shard_map/while/body/eval_jaxpr/dot_general | solution.py:143
  80.0 3.4 %all-to-all-start.2 = ((f32[4,128,128]{2,1,0:T(8,128)}), f32[4,128,128]{2,1,0:T(8,128)S(1)}, u32[]{:S(2)}, u32[]{:S(2)}) async-start(f32[4,128,128]{2,1,0:T(8,128)} %bitcast.36), calls=%async_computation.2 | async-start | bytes 524288 | tf_op jit(solution)/shard_map/all_to_all | solution.py:158
  83.5 6.6 %all-to-all-done.2 = f32[4,128,128]{2,1,0:T(8,128)S(1)} async-done(((f32[4,128,128]{2,1,0:T(8,128)}), f32[4,128,128]{2,1,0:T(8,128)S(1)}, u32[]{:S(2)}, u32[]{:S(2)}) %all-to-all-start.2) | async-done | bytes 262176 | tf_op jit(solution)/shard_map/all_to_all | solution.py:158
  90.1 1.6 gather_fusion
  91.8 119.1 %all-reduce.8.cloned.1.call-done = (f32[3,3,128,128]{3,2,1,0:T(8,128)}, f32[3,3,128,128]{3,2,1,0:T(8,128)}) async-done(((f32[3,3,128,128]{3,2,1,0:T(8,128)}, f32[3,3,128,128]{3,2,1,0:T(8,128)}), (f32[3,3,128,128]{3,2,1,0:T(8,128)}, f32[3,3,128,128]{3,2,1,0:T(8,128)})) %all-reduce.8.cloned.1.call-update) | async-done | bytes 1179664 | tf_op jit(solution)/shard_map/psum | solution.py:175
  210.9 2.0 broadcast_multiply_fusion.1
  212.9 0.9 broadcast_multiply_fusion
  (66 shorter events, 5.9 us)
Async XLA Ops:
  8.0 12.1 %copy-start.9 = (bf16[1,16,128,128]{3,2,1,0:T(8,128)(2,1)S(1)}, bf16[1,16,128,128]{3,2,1,0:T(8,128)(2,1)}, u32[]{:S(2)}) copy-start(bf16[1,16,128,128]{3,2,1,0:T(8,128)(2,1)} %param.12) | copy-start | bytes 1572868
  8.0 12.2 %copy-start.1 = (bf16[1,16,128,128]{3,2,1,0:T(8,128)(2,1)S(1)}, bf16[1,16,128,128]{3,2,1,0:T(8,128)(2,1)}, u32[]{:S(2)}) copy-start(bf16[1,16,128,128]{3,2,1,0:T(8,128)(2,1)} %param.13) | copy-start | bytes 1572868
  15.9 9.5 %all-to-all-start = ((s32[4,128,2]{1,2,0:T(2,128)}), s32[4,128,2]{1,2,0:T(2,128)S(1)}, u32[]{:S(2)}, u32[]{:S(2)}) async-start(s32[4,128,2]{1,2,0:T(2,128)} %copy.76), calls=%async_computation | async-start | bytes 8192 | tf_op jit(solution)/shard_map/all_to_all | solution.py:116
  20.1 2.0 copy-start.10
  20.1 2.1 copy-start.11
  20.3 9.0 %collective-permute-start.1 = (bf16[2,16,4,128]{3,2,1,0:T(4,128)(2,1)S(1)}, bf16[2,16,4,128]{3,2,1,0:T(4,128)(2,1)S(1)}, u32[]{:S(2)}, u32[]{:S(2)}) collective-permute-start(bf16[2,16,4,128]{3,2,1,0:T(4,128)(2,1)S(1)} %get-tuple-element.64), channel_id=1, source_target_pairs={{8,0},{16,8},{24,16},{0,24},{9,1},{17,9},{25,17},{1,25},{10,2},{18... | collective-permute-start | bytes 98312 | tf_op jit(solution)/shard_map/ppermute | solution.py:18
  22.1 7.2 %collective-permute-start = (bf16[2,16,4,128]{3,2,1,0:T(4,128)(2,1)S(1)}, bf16[2,16,4,128]{3,2,1,0:T(4,128)(2,1)S(1)}, u32[]{:S(2)}, u32[]{:S(2)}) collective-permute-start(bf16[2,16,4,128]{3,2,1,0:T(4,128)(2,1)S(1)} %get-tuple-element.63), channel_id=1, source_target_pairs={{0,8},{8,16},{16,24},{24,0},{1,9},{9,17},{17,25},{25,1},{2,10},{10... | collective-permute-start | bytes 98312 | tf_op jit(solution)/shard_map/ppermute | solution.py:17
  25.4 10.1 %all-to-all-start.1 = ((bf16[4,128,256]{2,1,0:T(8,128)(2,1)}), bf16[4,128,256]{2,1,0:T(8,128)(2,1)S(1)}, u32[]{:S(2)}, u32[]{:S(2)}) async-start(bf16[4,128,256]{2,1,0:T(8,128)(2,1)} %bitcast.13), calls=%async_computation.1 | async-start | bytes 524288 | tf_op jit(solution)/shard_map/all_to_all | solution.py:115
  28.8 182.1 %all-reduce.8.cloned.1.call-start = ((), (), s32[]{:S(2)}) async-start(), calls=%async_computation.5 | async-start | bytes 2359296 | tf_op jit(solution)/shard_map/psum | solution.py:175
  29.8 1.0 copy-start.3
  35.5 6.5 %copy-start.5 = (bf16[4,128,256]{2,1,0:T(8,128)(2,1)}, bf16[4,128,256]{2,1,0:T(8,128)(2,1)S(1)}, u32[]{:S(2)}) copy-start(bf16[4,128,256]{2,1,0:T(8,128)(2,1)S(1)} %all-to-all-done.1) | copy-start | bytes 786436
  59.2 3.4 %collective-permute-start.2 = (f32[16,3,128]{2,1,0:T(4,128)S(1)}, f32[16,3,128]{2,1,0:T(4,128)S(1)}, u32[]{:S(2)}, u32[]{:S(2)}) collective-permute-start(f32[16,3,128]{2,1,0:T(4,128)S(1)} %get-tuple-element.62), channel_id=1, source_target_pairs={{0,8},{8,16},{16,24},{24,0},{1,9},{9,17},{17,25},{25,1},{2,10},{10... | collective-permute-start | bytes 73736 | tf_op jit(solution)/shard_map/ppermute | solution.py:26
  60.2 3.2 %copy-start.4 = (bf16[3,3,128,128]{3,2,1,0:T(8,128)(2,1)S(1)}, bf16[3,3,128,128]{3,2,1,0:T(8,128)(2,1)}, u32[]{:S(2)}) copy-start(bf16[3,3,128,128]{3,2,1,0:T(8,128)(2,1)} %param.14) | copy-start | bytes 884740
  60.2 2.9 %collective-permute-start.3 = (f32[16,3,128]{2,1,0:T(4,128)S(1)}, f32[16,3,128]{2,1,0:T(4,128)S(1)}, u32[]{:S(2)}, u32[]{:S(2)}) collective-permute-start(f32[16,3,128]{2,1,0:T(4,128)S(1)} %get-tuple-element.61), channel_id=1, source_target_pairs={{0,24},{8,0},{16,8},{24,16},{1,25},{9,1},{17,9},{25,17},{2,26},{10... | collective-permute-start | bytes 73736 | tf_op jit(solution)/shard_map/ppermute | solution.py:26
  63.7 5.4 %collective-permute-start.5 = (bf16[16,1,128]{2,1,0:T(2,128)(2,1)S(1)}, bf16[16,1,128]{2,1,0:T(2,128)(2,1)S(1)}, u32[]{:S(2)}, u32[]{:S(2)}) collective-permute-start(bf16[16,1,128]{2,1,0:T(2,128)(2,1)S(1)} %get-tuple-element.66), channel_id=1, source_target_pairs={{8,0},{16,8},{24,16},{0,24},{9,1},{17,9},{25,17},{1,25},{10,2},{18... | collective-permute-start | bytes 12296 | tf_op jit(solution)/shard_map/ppermute | solution.py:18
  65.5 3.6 %collective-permute-start.4 = (bf16[16,1,128]{2,1,0:T(2,128)(2,1)S(1)}, bf16[16,1,128]{2,1,0:T(2,128)(2,1)S(1)}, u32[]{:S(2)}, u32[]{:S(2)}) collective-permute-start(bf16[16,1,128]{2,1,0:T(2,128)(2,1)S(1)} %get-tuple-element.65), channel_id=1, source_target_pairs={{0,8},{8,16},{16,24},{24,0},{1,9},{9,17},{17,25},{25,1},{2,10},{10... | collective-permute-start | bytes 12296 | tf_op jit(solution)/shard_map/ppermute | solution.py:17
  69.1 0.8 copy-start.6
  71.5 1.0 copy-start.2
  75.6 1.8 copy-start
  76.0 0.8 copy-start.7
  80.0 10.1 %all-to-all-start.2 = ((f32[4,128,128]{2,1,0:T(8,128)}), f32[4,128,128]{2,1,0:T(8,128)S(1)}, u32[]{:S(2)}, u32[]{:S(2)}) async-start(f32[4,128,128]{2,1,0:T(8,128)} %bitcast.36), calls=%async_computation.2 | async-start | bytes 524288 | tf_op jit(solution)/shard_map/all_to_all | solution.py:158
  83.4 130.3 %reduce-scatter.2.cloned.1.call-start = ((), (), s32[]{:S(2)}) async-start(), calls=%async_computation.4 | async-start | bytes 294912 | tf_op jit(solution)/shard_map/reduce_scatter | solution.py:160
  210.9 2.0 copy-start.8
Sparse Core Ops, SparseCore 0:
  77.0 133.8 all-reduce.7
Sparse Core Ops, SparseCore 1:
  91.8 62.9 reduce-scatter.1
where the time goes:
time: 222 us; the launch traced here: 221 us
  waiting for transfers between devices  127 us (57%)
  local copies, waits for them, and re-layouts  28.2 us (13%)
  matrix products  23.8 us (11%)
  starting transfers between devices  17.2 us (8%)
  between operations  16 us (7%)
  other arithmetic  8.87 us (4%)
    psum x1, waiting for transfers between devices, per_device(): lax.psum((first_term, second_term), ('lon', 'frame'))  119 us
    dot_general x1, local copies, waits for them, and re-layouts, block_step(): jnp.einsum('tir,tih->trh', row_hot, placed_cols, preferred_element_type=j...  7.86 us
    all_to_all x1, waiting for transfers between devices, per_device(): lax.all_to_all(slot_grads, 'lon', split_axis=0, concat_axis=0, tiled=True)  6.61 us
    dot_general x18, matrix products, weight_terms(): lax.dot_general(window, flat_grad, (((0,), (0,)), ((), ())), preferred_el...  6.16 us
    dot_general x1, matrix products, block_step(): jnp.einsum('tir,tih->trh', row_hot, placed_cols, preferred_element_type=j...  5.92 us
    dot_general x9, matrix products, conv_cells(): jnp.einsum('rci,io->rco', window, weight[row_tap, col_tap], preferred_ele...  4.72 us
  transfers between devices with their start and end apart: 11, of which 4 were waited for; matrix products, arithmetic and copies ran while one was open for 9% of the time, Pallas kernels for 0%

commit v1 on v0

--- a/solution.py
+++ b/solution.py
@@ -172,7 +172,7 @@
     )
     second_term = weight_terms(hidden_edged, feature_grad)
     first_term = weight_terms(input_edged, pre_grad)
-    first_sum, second_sum = lax.psum((first_term, second_term), ("lon", "frame"))
+    first_sum, second_sum = lax.psum(lax.psum((first_term, second_term), "frame"), "lon")
     norm_factor = 1.0 / math.sqrt(row_count * col_count * strip_count * lax.axis_size("frame"))
     return (query_grad, first_sum * norm_factor, second_sum * norm_factor)
 

time: 222 us -> 275 us (1.24)
  waiting for transfers between devices: 127 us -> 175 us
  matrix products: 23.8 us -> 27.9 us
    reduce_scatter x1, waiting for transfers between devices: 0.01 us -> 63.3 us  [per_device(): lax.psum_scatter(home_grads, 'frame', scatter_dimension=0, tiled=True)]
    psum x1 -> x2, waiting for transfers between devices: 119 us -> 103 us  [the longest x1 78.6 us: per_device(): lax.psum((first_term, second_term), 'frame')]
    dot_general x9, matrix products: 4.72 us -> 9.68 us  [conv_cells(): jnp.einsum('rci,io->rco', window, weight[row_tap, col_tap], preferred_ele...]
  transfers between devices with their start and end apart: 11 -> 12, of which waited for: 4 -> 5; matrix products, arithmetic and copies ran while one was open for 9% -> 9% of each run, Pallas kernels for 0% -> 0%
where the time goes in v1:
time: 275 us; the launch traced here: 274 us
  waiting for transfers between devices  175 us (64%)
  local copies, waits for them, and re-layouts  28.7 us (10%)
  matrix products  27.9 us (10%)
  starting transfers between devices  16.6 us (6%)
  between operations  14.3 us (5%)
  other arithmetic  10.9 us (4%)
    psum x1, waiting for transfers between devices, per_device(): lax.psum((first_term, second_term), 'frame')  78.6 us
    reduce_scatter x1, waiting for transfers between devices, per_device(): lax.psum_scatter(home_grads, 'frame', scatter_dimension=0, tiled=True)  63.3 us
    psum x1, waiting for transfers between devices, per_device(): lax.psum(lax.psum((first_term, second_term), 'frame'), 'lon')  24.2 us
    dot_general x9, matrix products, conv_cells(): jnp.einsum('rci,io->rco', window, weight[row_tap, col_tap], preferred_ele...  9.68 us
    all_to_all x1, waiting for transfers between devices, per_device(): lax.all_to_all(slot_grads, 'lon', split_axis=0, concat_axis=0, tiled=True)  8.4 us
    dot_general x1, local copies, waits for them, and re-layouts, block_step(): jnp.einsum('tir,tih->trh', row_hot, placed_cols, preferred_element_type=j...  7.87 us
    dot_general x18, matrix products, weight_terms(): lax.dot_general(window, flat_grad, (((0,), (0,)), ((), ())), preferred_el...  6.14 us
    dot_general x1, matrix products, block_step(): jnp.einsum('tir,tih->trh', row_hot, placed_cols, preferred_element_type=j...  5.9 us
  transfers between devices with their start and end apart: 12, of which 5 were waited for; matrix products, arithmetic and copies ran while one was open for 9% of the time, Pallas kernels for 0%

profile of v1, /device:TPU:0, one launch (start us, length us, event | category | flops | bytes accessed | tf_op | source)
XLA Modules:
  0.0 273.7 jit_solution(3359956333663298119)
XLA Ops:
  7.2 0.8 fusion.142
  8.0 1.2 reduce-window.6
  9.6 0.7 fusion.141
  10.3 0.7 compare_select_fusion
  11.0 0.7 add_bitcast_fusion.1
  11.7 0.7 pad_add_fusion
  12.6 1.8 scatter_custom_fusion
  14.3 0.7 copy.76
  15.1 4.2 %all-to-all-start = ((s32[4,128,2]{1,2,0:T(2,128)}), s32[4,128,2]{1,2,0:T(2,128)S(1)}, u32[]{:S(2)}, u32[]{:S(2)}) async-start(s32[4,128,2]{1,2,0:T(2,128)} %copy.76), calls=%async_computation | async-start | bytes 8192 | tf_op jit(solution)/shard_map/all_to_all | solution.py:116
  19.5 1.8 collective-permute-start.1
  21.6 3.0 %scatter_custom_fusion.1 = bf16[512,256]{1,0:T(8,128)(2,1)} fusion(s32[512]{0:T(512)S(1)} %bitcast.248, bf16[512,256]{1,0:T(8,128)(2,1)S(1)} %copy.78, bf16[]{:T(256)} %constant.86.clone.1), kind=kCustom, calls=%fused_computation.147 | custom fusion | bytes 262146 | tf_op jit(solution)/shard_map/scatter | solution.py:111
  24.6 3.4 %all-to-all-start.1 = ((bf16[4,128,256]{2,1,0:T(8,128)(2,1)}), bf16[4,128,256]{2,1,0:T(8,128)(2,1)S(1)}, u32[]{:S(2)}, u32[]{:S(2)}) async-start(bf16[4,128,256]{2,1,0:T(8,128)(2,1)} %bitcast.13), calls=%async_computation.1 | async-start | bytes 524288 | tf_op jit(solution)/shard_map/all_to_all | solution.py:115
  28.3 0.5 pad_maximum_fusion
  28.8 1.2 fusion.44
  30.1 1.2 convolution_add_fusion.7
  31.3 1.2 convolution_add_fusion.6
  32.5 2.2 convolution_add_fusion.5
  34.6 0.7 copy-done.6
  35.4 0.6 reshape.292
  36.0 5.9 %fusion.1 = bf16[512,16,134]{2,1,0:T(8,128)(2,1)} fusion(bf16[512,7,7]{2,1,0:T(8,128)(2,1)S(1)} %reshape.292, s32[512,7]{1,0:T(8,128)S(1)} %get-tuple-element.71, s32[512,7]{1,0:T(8,128)S(1)} %get-tuple-element.72), kind=kOutput, calls=%fused_computation.5 | convolution fusion | flops 23109632 | bytes 2274304 | tf_op jit(solution)/shard_map/while/body/eval_jaxpr/tir,tih->trh/dot_general | solution.py:139
  41.9 7.9 %copy.81 = bf16[512,16,134]{0,1,2:T(8,128)(2,1)} copy(bf16[512,16,134]{2,1,0:T(8,128)(2,1)} %fusion.1) | data formatting | bytes 4390912 | tf_op jit(solution)/shard_map/while/body/eval_jaxpr/tir,tih->trh/dot_general | solution.py:139
  49.7 2.8 %copy.83 = bf16[512,16,134]{0,2,1:T(8,128)(2,1)S(1)} copy(bf16[512,16,134]{0,1,2:T(8,128)(2,1)} %copy.81) | data formatting | bytes 4390912 | tf_op jit(solution)/shard_map/while/body/eval_jaxpr/convert_element_type | solution.py:141
  52.6 2.1 reshape.236
  54.7 2.6 dot_general.141
  57.3 1.7 fusion.97
  59.1 0.6 fusion.163
  59.7 0.5 collective-permute-start.2
  60.2 0.3 slice_bitcast_fusion
  60.7 1.5 collective-permute-start.3
  62.1 0.9 collective-permute-done.2
  63.0 0.6 slice_add_fusion.1
  63.7 0.9 scatter-add.6
  64.6 1.4 slice_add_fusion
  66.0 0.9 scatter-add.9
  67.3 1.3 collective-permute-start.5
  68.6 0.4 collective-permute-start.4
  68.9 0.3 fusion.20
  70.0 0.3 fusion.17
  70.3 0.3 fusion.16
  70.7 0.3 fusion.15
  71.0 0.3 fusion.14
  71.4 0.3 fusion.13
  71.7 0.3 fusion.12
  74.1 0.4 fusion.8
  76.6 0.3 fusion.25
  76.9 0.3 fusion.24
  77.3 0.3 fusion.23
  77.6 0.3 fusion.22
  78.0 0.3 fusion.21
  78.4 0.8 copy-done.8
  79.2 0.4 convolution_add_fusion.4
  79.7 0.4 convolution_add_fusion.3
  80.1 0.4 convolution_add_fusion.2
  80.6 0.4 convolution_add_fusion.1
  81.0 2.2 fusion.9
  83.2 78.6 %all-reduce.10.cloned.1.call-done = (f32[3,3,128,128]{3,2,1,0:T(8,128)}, f32[3,3,128,128]{3,2,1,0:T(8,128)}) async-done(((f32[3,3,128,128]{3,2,1,0:T(8,128)}, f32[3,3,128,128]{3,2,1,0:T(8,128)}), (f32[3,3,128,128]{3,2,1,0:T(8,128)}, f32[3,3,128,128]{3,2,1,0:T(8,128)})) %all-reduce.10.cloned.1.call-update) | async-done | bytes 1179664 | tf_op jit(solution)/shard_map/psum | solution.py:175
  161.9 1.5 fusion.46
  163.3 3.4 %all-to-all-start.2 = ((f32[4,128,128]{2,1,0:T(8,128)}), f32[4,128,128]{2,1,0:T(8,128)S(1)}, u32[]{:S(2)}, u32[]{:S(2)}) async-start(f32[4,128,128]{2,1,0:T(8,128)} %bitcast.36), calls=%async_computation.2 | async-start | bytes 524288 | tf_op jit(solution)/shard_map/all_to_all | solution.py:158
  166.8 8.4 %all-to-all-done.2 = f32[4,128,128]{2,1,0:T(8,128)S(1)} async-done(((f32[4,128,128]{2,1,0:T(8,128)}), f32[4,128,128]{2,1,0:T(8,128)S(1)}, u32[]{:S(2)}, u32[]{:S(2)}) %all-to-all-start.2) | async-done | bytes 262176 | tf_op jit(solution)/shard_map/all_to_all | solution.py:158
  175.2 1.6 gather_fusion
  176.9 24.2 %all-reduce.12.cloned.1.call-done = (f32[3,3,128,128]{3,2,1,0:T(8,128)}, f32[3,3,128,128]{3,2,1,0:T(8,128)}) async-done(((f32[3,3,128,128]{3,2,1,0:T(8,128)}, f32[3,3,128,128]{3,2,1,0:T(8,128)}), (f32[3,3,128,128]{3,2,1,0:T(8,128)}, f32[3,3,128,128]{3,2,1,0:T(8,128)})) %all-reduce.12.cloned.1.call-update) | async-done | bytes 1179664 | tf_op jit(solution)/shard_map/psum | solution.py:175
  201.0 2.0 broadcast_multiply_fusion.1
  203.0 0.9 broadcast_multiply_fusion
  203.9 63.3 %reduce-scatter.2.cloned.1.call-done = f32[64,128]{1,0:T(8,128)} async-done(((f32[512,128]{1,0:T(8,128)}), f32[64,128]{1,0:T(8,128)}) %reduce-scatter.2.cloned.1.call-update) | async-done | bytes 32784 | tf_op jit(solution)/shard_map/reduce_scatter | solution.py:160
  (73 shorter events, 6.7 us)
Async XLA Ops:
  7.2 12.1 %copy-start.11 = (bf16[1,16,128,128]{3,2,1,0:T(8,128)(2,1)S(1)}, bf16[1,16,128,128]{3,2,1,0:T(8,128)(2,1)}, u32[]{:S(2)}) copy-start(bf16[1,16,128,128]{3,2,1,0:T(8,128)(2,1)} %param.12) | copy-start | bytes 1572868
  7.2 12.2 %copy-start.4 = (bf16[1,16,128,128]{3,2,1,0:T(8,128)(2,1)S(1)}, bf16[1,16,128,128]{3,2,1,0:T(8,128)(2,1)}, u32[]{:S(2)}) copy-start(bf16[1,16,128,128]{3,2,1,0:T(8,128)(2,1)} %param.13) | copy-start | bytes 1572868
  15.1 9.5 %all-to-all-start = ((s32[4,128,2]{1,2,0:T(2,128)}), s32[4,128,2]{1,2,0:T(2,128)S(1)}, u32[]{:S(2)}, u32[]{:S(2)}) async-start(s32[4,128,2]{1,2,0:T(2,128)} %copy.76), calls=%async_computation | async-start | bytes 8192 | tf_op jit(solution)/shard_map/all_to_all | solution.py:116
  19.3 2.0 copy-start.12
  19.3 2.1 copy-start.13
  19.5 8.8 %collective-permute-start.1 = (bf16[2,16,4,128]{3,2,1,0:T(4,128)(2,1)S(1)}, bf16[2,16,4,128]{3,2,1,0:T(4,128)(2,1)S(1)}, u32[]{:S(2)}, u32[]{:S(2)}) collective-permute-start(bf16[2,16,4,128]{3,2,1,0:T(4,128)(2,1)S(1)} %get-tuple-element.66), channel_id=1, source_target_pairs={{8,0},{16,8},{24,16},{0,24},{9,1},{17,9},{25,17},{1,25},{10,2},{18... | collective-permute-start | bytes 98312 | tf_op jit(solution)/shard_map/ppermute | solution.py:18
  21.3 7.0 %collective-permute-start = (bf16[2,16,4,128]{3,2,1,0:T(4,128)(2,1)S(1)}, bf16[2,16,4,128]{3,2,1,0:T(4,128)(2,1)S(1)}, u32[]{:S(2)}, u32[]{:S(2)}) collective-permute-start(bf16[2,16,4,128]{3,2,1,0:T(4,128)(2,1)S(1)} %get-tuple-element.65), channel_id=1, source_target_pairs={{0,8},{8,16},{16,24},{24,0},{1,9},{9,17},{17,25},{25,1},{2,10},{10... | collective-permute-start | bytes 98312 | tf_op jit(solution)/shard_map/ppermute | solution.py:17
  24.6 10.1 %all-to-all-start.1 = ((bf16[4,128,256]{2,1,0:T(8,128)(2,1)}), bf16[4,128,256]{2,1,0:T(8,128)(2,1)S(1)}, u32[]{:S(2)}, u32[]{:S(2)}) async-start(bf16[4,128,256]{2,1,0:T(8,128)(2,1)} %bitcast.13), calls=%async_computation.1 | async-start | bytes 524288 | tf_op jit(solution)/shard_map/all_to_all | solution.py:115
  28.0 133.8 %all-reduce.10.cloned.1.call-start = ((), (), s32[]{:S(2)}) async-start(), calls=%async_computation.5 | async-start | bytes 2359296 | tf_op jit(solution)/shard_map/psum | solution.py:175
  28.8 1.3 copy-start.1
  34.6 0.7 copy-start.6
  57.3 2.9 %copy-start.2 = (bf16[2,16,136,128]{3,2,1,0:T(8,128)(2,1)S(1)}, bf16[2,16,136,128]{3,2,1,0:T(8,128)(2,1)}, u32[]{:S(2)}) copy-start(bf16[2,16,136,128]{3,2,1,0:T(8,128)(2,1)} %copy-done.1) | copy-start | bytes 3342340
  59.7 3.3 %collective-permute-start.2 = (f32[16,3,128]{2,1,0:T(4,128)S(1)}, f32[16,3,128]{2,1,0:T(4,128)S(1)}, u32[]{:S(2)}, u32[]{:S(2)}) collective-permute-start(f32[16,3,128]{2,1,0:T(4,128)S(1)} %get-tuple-element.64), channel_id=1, source_target_pairs={{0,8},{8,16},{16,24},{24,0},{1,9},{9,17},{17,25},{25,1},{2,10},{10... | collective-permute-start | bytes 73736 | tf_op jit(solution)/shard_map/ppermute | solution.py:26
  60.7 6.3 %copy-start.5 = (bf16[3,3,128,128]{3,2,1,0:T(8,128)(2,1)S(1)}, bf16[3,3,128,128]{3,2,1,0:T(8,128)(2,1)}, u32[]{:S(2)}) copy-start(bf16[3,3,128,128]{3,2,1,0:T(8,128)(2,1)} %param.14) | copy-start | bytes 884740
  60.7 3.9 %collective-permute-start.3 = (f32[16,3,128]{2,1,0:T(4,128)}, f32[16,3,128]{2,1,0:T(4,128)}, u32[]{:S(2)}, u32[]{:S(2)}) collective-permute-start(f32[16,3,128]{2,1,0:T(4,128)} %get-tuple-element.63), channel_id=1, source_target_pairs={{0,24},{8,0},{16,8},{24,16},{1,25},{9,1},{17,9},{25,17},{2,26},{10... | collective-permute-start | bytes 73736 | tf_op jit(solution)/shard_map/ppermute | solution.py:26
  67.3 4.8 %collective-permute-start.5 = (bf16[16,1,128]{2,1,0:T(2,128)(2,1)S(1)}, bf16[16,1,128]{2,1,0:T(2,128)(2,1)S(1)}, u32[]{:S(2)}, u32[]{:S(2)}) collective-permute-start(bf16[16,1,128]{2,1,0:T(2,128)(2,1)S(1)} %get-tuple-element.68), channel_id=1, source_target_pairs={{8,0},{16,8},{24,16},{0,24},{9,1},{17,9},{25,17},{1,25},{10,2},{18... | collective-permute-start | bytes 12296 | tf_op jit(solution)/shard_map/ppermute | solution.py:18
  68.6 3.5 %collective-permute-start.4 = (bf16[16,1,128]{2,1,0:T(2,128)(2,1)S(1)}, bf16[16,1,128]{2,1,0:T(2,128)(2,1)S(1)}, u32[]{:S(2)}, u32[]{:S(2)}) collective-permute-start(bf16[16,1,128]{2,1,0:T(2,128)(2,1)S(1)} %get-tuple-element.67), channel_id=1, source_target_pairs={{0,8},{8,16},{16,24},{24,0},{1,9},{9,17},{17,25},{25,1},{2,10},{10... | collective-permute-start | bytes 12296 | tf_op jit(solution)/shard_map/ppermute | solution.py:17
  72.1 0.8 copy-start.7
  78.0 1.3 copy-start.3
  78.3 0.8 copy-start.8
  79.2 121.9 %all-reduce.12.cloned.1.call-start = ((), (), s32[]{:S(2)}) async-start(), calls=%async_computation.6 | async-start | bytes 2359296 | tf_op jit(solution)/shard_map/psum | solution.py:175
  81.0 80.8 %copy-start = (bf16[512,16,134]{0,1,2:T(8,128)(2,1)S(1)}, bf16[512,16,134]{0,1,2:T(8,128)(2,1)}, u32[]{:S(2)}) copy-start(bf16[512,16,134]{0,1,2:T(8,128)(2,1)} %copy.81) | copy-start | bytes 6586372
  83.2 78.7 %copy-start.10 = (bf16[16,134,128]{2,1,0:T(8,128)(2,1)S(1)}, bf16[16,134,128]{2,1,0:T(8,128)(2,1)}, u32[]{:S(2)}) copy-start(bf16[16,134,128]{2,1,0:T(8,128)(2,1)} %fusion.9) | copy-start | bytes 1646596
  163.3 11.9 %all-to-all-start.2 = ((f32[4,128,128]{2,1,0:T(8,128)}), f32[4,128,128]{2,1,0:T(8,128)S(1)}, u32[]{:S(2)}, u32[]{:S(2)}) async-start(f32[4,128,128]{2,1,0:T(8,128)} %bitcast.36), calls=%async_computation.2 | async-start | bytes 524288 | tf_op jit(solution)/shard_map/all_to_all | solution.py:158
  166.8 100.5 %reduce-scatter.2.cloned.1.call-start = ((), (), s32[]{:S(2)}) async-start(), calls=%async_computation.4 | async-start | bytes 294912 | tf_op jit(solution)/shard_map/reduce_scatter | solution.py:160
  201.0 2.0 copy-start.9
Sparse Core Ops, SparseCore 0:
  79.3 82.4 all-reduce.9
  164.2 36.7 all-reduce.11
  204.9 62.2 reduce-scatter.1
